TPU v7x, 256 devices: a whole 4x4x8 slice. The times are simulated.
256 devices in a mesh: row: 16 (over z, y_lo), col: 16 (over x, y_hi, core).
Axes of the slice: x: 4, y: 4 (y_hi: 2, y_lo: 2; y = y_hi * 2 + y_lo), z: 8, core: 2. Of those that a mesh axis runs over, the one named last changes fastest.
Arguments:
- raw: int32 [32768, 4096], P('col', 'row'), may hold values from -128 to 127
- taps: int32 [16, 128], replicated, may hold values from -256 to 256
Outputs:
- visibility: bfloat16 [32, 4096, 2, 4096], P(None, 'row', None, 'col')
All inputs are finite; a program needn't handle non-finite values.
Results may differ from a plain program's by a relative error of at most 0.0056.
Values may be sent and summed in bfloat16 or wider, within the bound.
A program may use at most 128 MiB of HBM per device.

v0:
```python
import math
import jax
import jax.numpy as jnp
from jax import lax
from jax.sharding import PartitionSpec as P

CHANNELS = 32
TRANSFORM = 128
TAPS = 16
SPECTRA_DEV = 16
BLOCKS = 2


def from_behind(block, axis, distance):
    devices = range(lax.axis_size(axis))
    route = [(i - distance, i) for i in devices if i - distance in devices]
    return lax.ppermute(block, axis, route)


def from_root(value, axis, root):
    mine = lax.axis_index(axis) == root
    return lax.psum(jnp.where(mine, value, jnp.zeros_like(value)), axis)


def dft_table():
    sample = jnp.arange(TRANSFORM, dtype=jnp.int32)[:, None]
    channel = jnp.arange(1, CHANNELS + 1, dtype=jnp.int32)[None, :]
    phase = (sample * channel % TRANSFORM).astype(jnp.float32) * (2.0 * math.pi / TRANSFORM)
    return jnp.concatenate([jnp.cos(phase), -jnp.sin(phase)], axis=1)


def channelize(extended, taps, count):
    coeffs = taps.astype(jnp.float32)
    weighted = jnp.zeros((count, TRANSFORM, extended.shape[2]), jnp.float32)
    for offset in range(TAPS):
        start = TAPS - 1 - offset
        weighted = weighted + coeffs[offset][None, :, None] * extended[
            start : start + count
        ].astype(jnp.float32)
    scale = 1.0 / (8192.0 * math.sqrt(TAPS * TRANSFORM))
    spectra = (
        jnp.einsum("sni,nk->ksi", weighted, dft_table(), precision=lax.Precision.HIGHEST) * scale
    )
    return spectra.reshape(2, CHANNELS, count, extended.shape[2]).astype(jnp.bfloat16)


def correlate(row_block, column_block):
    spectra_all = row_block.shape[2]
    width = spectra_all // BLOCKS
    total = None
    for block in range(BLOCKS):
        left = jnp.concatenate(
            [
                row_block[0, :, block * width : (block + 1) * width],
                row_block[1, :, block * width : (block + 1) * width],
            ],
            axis=1,
        )
        real_part = column_block[0, :, block * width : (block + 1) * width]
        imag_part = column_block[1, :, block * width : (block + 1) * width]
        right = jnp.concatenate(
            [
                jnp.concatenate([real_part, imag_part], axis=1),
                jnp.concatenate([-imag_part, real_part], axis=1),
            ],
            axis=2,
        )
        term = lax.dot_general(
            left, right, (((1,), (1,)), ((0,), (0,))), preferred_element_type=jnp.float32
        )
        if block == 0:
            total = term
        else:
            summed = total + term
            total = summed
    result = (total * (1.0 / spectra_all)).astype(jnp.bfloat16)
    return result.reshape(CHANNELS, row_block.shape[3], 2, column_block.shape[3])


def body(raw, taps):
    frames = raw.astype(jnp.bfloat16).reshape(SPECTRA_DEV, TRANSFORM, raw.shape[1])
    rim_frames = frames[SPECTRA_DEV - (TAPS - 1) :]
    earlier = from_behind(rim_frames, "col", 1)
    extended = jnp.concatenate([earlier, frames], axis=0)
    pieces = channelize(extended, taps, SPECTRA_DEV)
    row_block = lax.all_gather(pieces, "col", axis=2, tiled=True)
    ratio = lax.axis_size("row") // lax.axis_size("col")
    first_root = lax.axis_index("col") * ratio
    received = from_root(row_block, "row", first_root + 0)
    return correlate(row_block, received)


def solution(mesh):
    placed = (P("col", "row"), P())
    return jax.shard_map(
        body, mesh=mesh, in_specs=placed, out_specs=P(None, "row", None, "col"), check_vma=False
    )
```

profile of v0, /device:TPU:1, one launch (start us, length us, event | category | flops | bytes accessed | tf_op | source)
XLA Modules:
  0.0 541.9 jit_solution(9237460583808072064)
XLA Ops:
  6.5 0.0 copy-start.1
  6.5 0.0 all-gather.2.cloned.1.call-start
  6.5 1.8 convert_element_type.70
  8.3 0.1 slice.166
  8.4 6.2 %collective-permute-start = (bf16[15,128,256]{2,1,0:T(8,128)(2,1)S(1)}, bf16[15,128,256]{2,1,0:T(8,128)(2,1)S(1)}, u32[]{:S(2)}, u32[]{:S(2)}) collective-permute-start(bf16[15,128,256]{2,1,0:T(8,128)(2,1)S(1)} %bitcast.59), channel_id=1, source_target_pairs={{0,1},{1,2},{2,3},{3,4},{4,5},{5,6},{6,7},{7,8},{8,9},{9,10},{10,1... | collective-permute-start | bytes 2949128 | tf_op jit(solution)/shard_map/ppermute | solution.py:17
  14.6 0.0 copy-done.1
  14.7 0.2 fusion.128
  14.8 10.8 %collective-permute-done = bf16[15,128,256]{2,1,0:T(8,128)(2,1)S(1)} collective-permute-done((bf16[15,128,256]{2,1,0:T(8,128)(2,1)S(1)}, bf16[15,128,256]{2,1,0:T(8,128)(2,1)S(1)}, u32[]{:S(2)}, u32[]{:S(2)}) %collective-permute-start) | collective-permute-done | bytes 983072 | tf_op jit(solution)/shard_map/ppermute | solution.py:17
  25.6 5.2 fusion.72
  30.8 1.1 copy.3
  31.9 0.0 all-gather.2.cloned.1.call-update
  31.9 0.0 all-reduce.2.cloned.1.call-start
  32.0 89.2 %all-gather.2.cloned.1.call-done = bf16[2,32,256,256]{3,2,1,0:T(8,128)(2,1)} async-done(((bf16[2,32,16,256]{3,2,1,0:T(8,128)(2,1)}), bf16[2,32,256,256]{3,2,1,0:T(8,128)(2,1)}) %all-gather.2.cloned.1.call-update) | async-done | bytes 8388624 | tf_op jit(solution)/shard_map/all_gather | solution.py:86
  121.2 3.9 broadcast_select_fusion
  125.1 0.0 all-reduce.2.cloned.1.call-update
  125.1 5.6 %slice_bitcast_fusion.3 = (bf16[32,128,256]{2,1,0:T(8,128)(2,1)S(1)}, bf16[32,128,256]{2,1,0:T(8,128)(2,1)}, bf16[32,128,256]{2,1,0:T(8,128)(2,1)}, bf16[32,128,256]{2,1,0:T(8,128)(2,1)}) fusion(bf16[2,32,256,256]{3,2,1,0:T(8,128)(2,1)} %all-gather.2.cloned.1.call-done), kind=kLoop, calls=%fused_computation.54 | loop fusion | bytes 16777216 | tf_op jit(solution)/shard_map/squeeze | solution.py:54
  130.8 361.4 %all-reduce.2.cloned.1.call-done = bf16[2,32,256,256]{3,2,1,0:T(8,128)(2,1)} async-done(((bf16[2,32,256,256]{3,2,1,0:T(8,128)(2,1)}), bf16[2,32,256,256]{3,2,1,0:T(8,128)(2,1)}) %all-reduce.2.cloned.1.call-update) | async-done | bytes 8388624 | tf_op jit(solution)/shard_map/psum | solution.py:22
  492.2 0.0 copy-start
  492.2 2.6 fusion.134
  494.8 2.0 copy-done
  496.8 3.4 slice_bitcast_fusion
  500.3 10.2 %fusion = f32[32,256,512]{2,1,0:T(8,128)} fusion(bf16[32,128,256]{2,1,0:T(8,128)(2,1)} %get-tuple-element.12, bf16[32,128,256]{2,1,0:T(8,128)(2,1)S(1)} %get-tuple-element.14, bf16[32,128,256]{2,1,0:T(8,128)(2,1)} %get-tuple-element.11, bf16[32,128,256]{2,1,0:T(8,128)(2,1)} %get-tuple-element.7, bf16[32,128,256]{2,1,0:T(8,128)(2,1)} %get-tuple-element.8), kind=kOutput, calls=%fused_computation.1 | convolution fusion | flops 2189426688 | bytes 27262976 | tf_op jit(solution)/shard_map/dot_general | solution.py:68
  510.5 12.1 %multiply_convert_fusion = bf16[32,256,512]{2,1,0:T(8,128)(2,1)} fusion(f32[32,256,512]{2,1,0:T(8,128)} %fusion, bf16[32,128,256]{2,1,0:T(8,128)(2,1)} %get-tuple-element.10, bf16[32,128,256]{2,1,0:T(8,128)(2,1)S(1)} %get-tuple-element.13, bf16[32,128,256]{2,1,0:T(8,128)(2,1)} %get-tuple-element.9, bf16[32,128,256]{2,1,0:T(8,128)(2,1)} %get-tuple-element.6, ...), kind=kOutput, calls=%fused_computation | convolution fusion | flops 2202009600 | bytes 35651584 | tf_op jit(solution)/shard_map/dot_general | solution.py:68
  522.6 12.5 %reshape.30 = bf16[32,256,2,256]{3,2,1,0:T(2,128)(2,1)} reshape(bf16[32,256,512]{2,1,0:T(8,128)(2,1)} %multiply_convert_fusion) | data formatting | bytes 16777216 | tf_op jit(solution)/shard_map/reshape | solution.py:77
  (3 shorter events, 0.0 us)
Async XLA Ops:
  6.5 8.1 %copy-start.1 = (s32[16,128]{1,0:T(8,128)S(1)}, s32[16,128]{1,0:T(8,128)}, u32[]{:S(2)}) copy-start(s32[16,128]{1,0:T(8,128)} %param.3) | copy-start | bytes 24580
  6.5 114.6 %all-gather.2.cloned.1.call-start = ((), (), s32[]{:S(2)}) async-start(), calls=%async_computation | async-start | bytes 8912896 | tf_op jit(solution)/shard_map/all_gather | solution.py:86
  8.4 17.2 %collective-permute-start = (bf16[15,128,256]{2,1,0:T(8,128)(2,1)S(1)}, bf16[15,128,256]{2,1,0:T(8,128)(2,1)S(1)}, u32[]{:S(2)}, u32[]{:S(2)}) collective-permute-start(bf16[15,128,256]{2,1,0:T(8,128)(2,1)S(1)} %bitcast.59), channel_id=1, source_target_pairs={{0,1},{1,2},{2,3},{3,4},{4,5},{5,6},{6,7},{7,8},{8,9},{9,10},{10,1... | collective-permute-start | bytes 2949128 | tf_op jit(solution)/shard_map/ppermute | solution.py:17
  31.9 460.3 %all-reduce.2.cloned.1.call-start = ((), (), s32[]{:S(2)}) async-start(), calls=%async_computation.1 | async-start | bytes 16777216 | tf_op jit(solution)/shard_map/psum | solution.py:22
  492.2 4.6 copy-start
Sparse Core Ops, SparseCore 0:
  32.0 89.1 all-gather.1
  125.3 366.8 all-reduce.1
where the time goes:
time: 542 us
  waiting for transfers between devices  461 us (85%)
  matrix products  27.5 us (5%)
  local copies, waits for them, and re-layouts  24.7 us (5%)
  between operations  13.5 us (2%)
  other arithmetic  8.52 us (2%)
  starting transfers between devices  6.26 us (1%)
    psum x1, waiting for transfers between devices, from_root(): return lax.psum(jnp.where(mine, value, jnp.zeros_like(value)), axis)  361 us
    all_gather x1, waiting for transfers between devices, body(): row_block = lax.all_gather(pieces, 'col', axis=2, tiled=True)  89.2 us
    dot_general x2, matrix products, correlate(): lax.dot_general(left, right, (((1,), (1,)), ((0,), (0,))), preferred_elem...  22.3 us
    reshape x1, local copies, waits for them, and re-layouts, correlate(): result.reshape(CHANNELS, row_block.shape[3], 2, column_block.shape[3])  12.5 us
  transfers between devices with their start and end apart: 3, of which 3 were waited for; matrix products, arithmetic and copies ran while one was open for 1% of the time, Pallas kernels for 0%

commit v1 on v0

--- a/solution.py
+++ b/solution.py
@@ -83,7 +83,9 @@
     earlier = from_behind(rim_frames, "col", 1)
     extended = jnp.concatenate([earlier, frames], axis=0)
     pieces = channelize(extended, taps, SPECTRA_DEV)
-    row_block = lax.all_gather(pieces, "col", axis=2, tiled=True)
+    row_block = jnp.concatenate(
+        lax.all_to_all(jnp.stack([pieces] * lax.axis_size("col")), "col", 0, 0), axis=2
+    )
     ratio = lax.axis_size("row") // lax.axis_size("col")
     first_root = lax.axis_index("col") * ratio
     received = from_root(row_block, "row", first_root + 0)

time: 542 us -> 612 us (1.13)
  waiting for transfers between devices: 461 us -> 508 us
  local copies, waits for them, and re-layouts: 24.7 us -> 36.3 us
  starting transfers between devices: 6.26 us -> 14.4 us
    all_to_all x0 -> x1, waiting for transfers between devices: none -> 131 us  [body(): lax.all_to_all(jnp.stack([pieces] * lax.axis_size('col')), 'col', 0, 0)]
    all_gather x1 -> x0, waiting for transfers between devices: 89.2 us -> none  [body(): row_block = lax.all_gather(pieces, 'col', axis=2, tiled=True)]
    all_to_all x0 -> x1, starting transfers between devices: none -> 8.13 us  [body(): lax.all_to_all(jnp.stack([pieces] * lax.axis_size('col')), 'col', 0, 0)]
    reshape x0 -> x1, local copies, waits for them, and re-layouts: none -> 8.01 us  [body(): jnp.concatenate(lax.all_to_all(jnp.stack([pieces] * lax.axis_size('col'))...]
where the time goes in v1:
time: 612 us; the launch traced here: 611 us
  waiting for transfers between devices  508 us (83%)
  local copies, waits for them, and re-layouts  36.3 us (6%)
  matrix products  27.5 us (4%)
  starting transfers between devices  14.4 us (2%)
  between operations  13.5 us (2%)
  other arithmetic  11.7 us (2%)
    psum x1, waiting for transfers between devices, from_root(): return lax.psum(jnp.where(mine, value, jnp.zeros_like(value)), axis)  366 us
    all_to_all x1, waiting for transfers between devices, body(): lax.all_to_all(jnp.stack([pieces] * lax.axis_size('col')), 'col', 0, 0)  131 us
    dot_general x2, matrix products, correlate(): lax.dot_general(left, right, (((1,), (1,)), ((0,), (0,))), preferred_elem...  22.4 us
    reshape x1, local copies, waits for them, and re-layouts, correlate(): result.reshape(CHANNELS, row_block.shape[3], 2, column_block.shape[3])  12.5 us
  transfers between devices with their start and end apart: 3, of which 3 were waited for; matrix products, arithmetic and copies ran while one was open for 1% of the time, Pallas kernels for 0%

profile of v1, /device:TPU:1, one launch (start us, length us, event | category | flops | bytes accessed | tf_op | source)
XLA Modules:
  0.0 611.5 jit_solution(6307441385178613243)
XLA Ops:
  6.5 0.0 copy-start.1
  6.5 1.8 convert_element_type.72
  8.3 0.1 slice.166
  8.4 6.2 %collective-permute-start = (bf16[15,128,256]{2,1,0:T(8,128)(2,1)S(1)}, bf16[15,128,256]{2,1,0:T(8,128)(2,1)S(1)}, u32[]{:S(2)}, u32[]{:S(2)}) collective-permute-start(bf16[15,128,256]{2,1,0:T(8,128)(2,1)S(1)} %bitcast.63), channel_id=1, source_target_pairs={{0,1},{1,2},{2,3},{3,4},{4,5},{5,6},{6,7},{7,8},{8,9},{9,10},{10,1... | collective-permute-start | bytes 2949128 | tf_op jit(solution)/shard_map/ppermute | solution.py:17
  14.6 0.0 copy-done.1
  14.7 0.2 fusion.128
  14.8 10.8 %collective-permute-done = bf16[15,128,256]{2,1,0:T(8,128)(2,1)S(1)} collective-permute-done((bf16[15,128,256]{2,1,0:T(8,128)(2,1)S(1)}, bf16[15,128,256]{2,1,0:T(8,128)(2,1)S(1)}, u32[]{:S(2)}, u32[]{:S(2)}) %collective-permute-start) | collective-permute-done | bytes 983072 | tf_op jit(solution)/shard_map/ppermute | solution.py:17
  25.6 5.2 fusion.72
  30.8 0.3 copy.6
  31.1 4.3 stack.2
  35.4 8.1 %all-to-all-start = ((bf16[16,2,32,16,256]{4,3,2,1,0:T(8,128)(2,1)}), bf16[16,2,32,16,256]{4,3,2,1,0:T(8,128)(2,1)}, u32[]{:S(2)}, u32[]{:S(2)}) async-start(bf16[16,2,32,16,256]{4,3,2,1,0:T(8,128)(2,1)} %stack.2), calls=%async_computation | async-start | bytes 16777216 | tf_op jit(solution)/shard_map/all_to_all | solution.py:87
  43.6 0.0 all-reduce.2.cloned.1.call-start
  43.6 131.4 %all-to-all-done = bf16[16,2,32,16,256]{4,3,2,1,0:T(8,128)(2,1)} async-done(((bf16[16,2,32,16,256]{4,3,2,1,0:T(8,128)(2,1)}), bf16[16,2,32,16,256]{4,3,2,1,0:T(8,128)(2,1)}, u32[]{:S(2)}, u32[]{:S(2)}) %all-to-all-start) | async-done | bytes 8388640 | tf_op jit(solution)/shard_map/all_to_all | solution.py:87
  175.0 8.0 %copy.7 = bf16[2,32,16,16,256]{4,3,2,1,0:T(8,128)(2,1)} copy(bf16[2,32,16,16,256]{4,3,1,0,2:T(8,128)(2,1)} %bitcast.20) | data formatting | bytes 16777216 | tf_op jit(solution)/shard_map/reshape | solution.py:86
  183.1 7.2 %broadcast_select_fusion = bf16[2,32,256,256]{3,2,1,0:T(8,128)(2,1)} fusion(pred[]{:T(512)S(6)} %eq.5, bf16[2,32,16,16,256]{4,3,2,1,0:T(8,128)(2,1)} %copy.7), kind=kLoop, calls=%fused_computation.16 | loop fusion | flops 4194304 | bytes 16777216 | tf_op jit(solution)/shard_map/jit(_where)/select_n | solution.py:22
  190.2 0.0 all-reduce.2.cloned.1.call-update
  190.2 5.6 slice_bitcast_fusion.3
  195.9 365.8 %all-reduce.2.cloned.1.call-done = bf16[2,32,256,256]{3,2,1,0:T(8,128)(2,1)} async-done(((bf16[2,32,256,256]{3,2,1,0:T(8,128)(2,1)}), bf16[2,32,256,256]{3,2,1,0:T(8,128)(2,1)}) %all-reduce.2.cloned.1.call-update) | async-done | bytes 8388624 | tf_op jit(solution)/shard_map/psum | solution.py:22
  561.7 0.0 copy-start
  561.7 2.6 fusion.134
  564.3 2.0 copy-done
  566.3 3.5 slice_bitcast_fusion
  569.8 10.2 %fusion = f32[32,256,512]{2,1,0:T(8,128)} fusion(bf16[32,128,256]{2,1,0:T(8,128)(2,1)} %get-tuple-element.12, bf16[32,128,256]{2,1,0:T(8,128)(2,1)S(1)} %get-tuple-element.14, bf16[32,128,256]{2,1,0:T(8,128)(2,1)} %get-tuple-element.11, bf16[32,128,256]{2,1,0:T(8,128)(2,1)} %get-tuple-element.7, bf16[32,128,256]{2,1,0:T(8,128)(2,1)} %get-tuple-element.8), kind=kOutput, calls=%fused_computation.1 | convolution fusion | flops 2189426688 | bytes 27262976 | tf_op jit(solution)/shard_map/dot_general | solution.py:68
  580.0 12.1 %multiply_convert_fusion = bf16[32,256,512]{2,1,0:T(8,128)(2,1)} fusion(f32[32,256,512]{2,1,0:T(8,128)} %fusion, bf16[32,128,256]{2,1,0:T(8,128)(2,1)} %get-tuple-element.10, bf16[32,128,256]{2,1,0:T(8,128)(2,1)S(1)} %get-tuple-element.13, bf16[32,128,256]{2,1,0:T(8,128)(2,1)} %get-tuple-element.9, bf16[32,128,256]{2,1,0:T(8,128)(2,1)} %get-tuple-element.6, ...), kind=kOutput, calls=%fused_computation | convolution fusion | flops 2202009600 | bytes 35651584 | tf_op jit(solution)/shard_map/dot_general | solution.py:68
  592.1 12.5 %reshape.41 = bf16[32,256,2,256]{3,2,1,0:T(2,128)(2,1)} reshape(bf16[32,256,512]{2,1,0:T(8,128)(2,1)} %multiply_convert_fusion) | data formatting | bytes 16777216 | tf_op jit(solution)/shard_map/reshape | solution.py:77
  (3 shorter events, 0.0 us)
Async XLA Ops:
  6.5 8.1 %copy-start.1 = (s32[16,128]{1,0:T(8,128)S(1)}, s32[16,128]{1,0:T(8,128)}, u32[]{:S(2)}) copy-start(s32[16,128]{1,0:T(8,128)} %param.3) | copy-start | bytes 24580
  8.4 17.2 %collective-permute-start = (bf16[15,128,256]{2,1,0:T(8,128)(2,1)S(1)}, bf16[15,128,256]{2,1,0:T(8,128)(2,1)S(1)}, u32[]{:S(2)}, u32[]{:S(2)}) collective-permute-start(bf16[15,128,256]{2,1,0:T(8,128)(2,1)S(1)} %bitcast.63), channel_id=1, source_target_pairs={{0,1},{1,2},{2,3},{3,4},{4,5},{5,6},{6,7},{7,8},{8,9},{9,10},{10,1... | collective-permute-start | bytes 2949128 | tf_op jit(solution)/shard_map/ppermute | solution.py:17
  35.4 139.6 %all-to-all-start = ((bf16[16,2,32,16,256]{4,3,2,1,0:T(8,128)(2,1)}), bf16[16,2,32,16,256]{4,3,2,1,0:T(8,128)(2,1)}, u32[]{:S(2)}, u32[]{:S(2)}) async-start(bf16[16,2,32,16,256]{4,3,2,1,0:T(8,128)(2,1)} %stack.2), calls=%async_computation | async-start | bytes 16777216 | tf_op jit(solution)/shard_map/all_to_all | solution.py:87
  43.6 518.1 %all-reduce.2.cloned.1.call-start = ((), (), s32[]{:S(2)}) async-start(), calls=%async_computation.1 | async-start | bytes 16777216 | tf_op jit(solution)/shard_map/psum | solution.py:22
  561.7 4.6 copy-start
Sparse Core Ops, SparseCore 0:
  190.4 371.2 all-reduce.1
